TPU v7x, 32 devices: a whole 2x2x4 slice. The times are simulated.
32 devices in a mesh: by: 4 (over y, x), bx: 8 (over z, core).
Axes of the slice: x: 2, y: 2, z: 4, core: 2. Of those that a mesh axis runs over, the one named last changes fastest.
Arguments:
- tracers: float32 [2, 8, 384, 1024], P(None, None, 'by', 'bx'), may hold values from -6 to 6
- velocity: float32 [2, 8, 384, 1024], P(None, None, 'by', 'bx'), may hold values from -0.4 to 0.4
- diffusivity: float32 [8, 384, 1024], P(None, 'by', 'bx'), may hold values from 0.02 to 0.2
- kmt: int32 [384, 1024], P('by', 'bx'), may hold values from 0 to 8
- forcing: float32 [384, 1024], P('by', 'bx'), may hold values from -6 to 6
- free_surface: float32 [384, 1024], P('by', 'bx'), may hold values from 0.25 to 2
Outputs:
- new_tracers: float32 [2, 8, 384, 1024], P(None, None, 'by', 'bx')
- surface: float32 [384, 1024], P('by', 'bx')
- residual: float32 [384, 1024], P('by', 'bx')
All inputs are finite; a program needn't handle non-finite values.
Results may differ from a plain program's by a relative error of at most 0.0003.
Values sent between devices are 32-bit elements; how exact they have to be, the bound alone decides.
No kernel may reach another device: no remote copies, remote signals or barrier semaphores. Data moves between devices by JAX's collectives and lax.ppermute only.
A program may use at most 64 MiB of HBM per device.

v0:
```python
import jax
import jax.numpy as jnp
from jax import lax
from jax.experimental import pallas as pl
from jax.experimental.pallas import tpu as pltpu
from jax.sharding import PartitionSpec as P


AXES = ("by", "bx")
ITERS = 4
TILE = 8
REACH = 4
CENTER = 5.0
HALFWIDTH = 4.0
VMEM_GRANT = 12 << 20
LIMIT = 1000.0


def lanes_of(shape):
    return lax.broadcasted_iota(jnp.int32, shape, 1)


def rows_of(shape):
    return lax.broadcasted_iota(jnp.int32, shape, 0)


def roll(value, shift, axis=1):
    size = value.shape[axis]
    shift = shift % size
    return value if shift == 0 else pltpu.roll(value, shift, axis)


def grouped_sum(value, first, last):
    step = first
    while step < last:
        value = value + roll(value, step)
        step *= 2
    return value


def unfold(block, rows, levels):
    half = block[: rows // 2]
    return jnp.concatenate([half, roll(half, -(6 * levels + 16))], axis=0)


def level_terms(kmt, k, di, u, v):
    wet = kmt > k
    mixing = jnp.where(wet, di, 0.0)
    across = jnp.where(wet, 0.5 * u, 0.0)
    along = jnp.where(wet, 0.5 * v, 0.0)
    return wet, 1.0 - 4.0 * mixing, mixing - across, mixing + across, mixing - along, mixing + along


def within(value, own, c_east, c_west, c_north, c_south):
    return (
        value * own
        + c_east * roll(value, -1)
        + c_west * roll(value, 1)
        + c_north * roll(value, -1, 0)
        + c_south * roll(value, 1, 0)
    )


def inside(c_east, c_west, c_north, c_south, lane, row):
    rows, cols = lane.shape
    return (
        jnp.where(lane == cols - 1, 0.0, c_east),
        jnp.where(lane == 0, 0.0, c_west),
        jnp.where(row == rows - 1, 0.0, c_north),
        jnp.where(row == 0, 0.0, c_south),
    )


def stencil_kernel(
    tr_hbm, ve_hbm, di_hbm, kmt_hbm, fo_hbm, fs_hbm, packed, top, bottom, rhs_out, weight, tr, ve, di, kmt_ref, fs, fo, sems, flat_sems
):
    levels = tr.shape[1]
    rows, cols = kmt_ref.shape
    chunk = rows // 2
    flat = [
        pltpu.make_async_copy(source, target, flat_sems.at[i])
        for i, (source, target) in enumerate(((kmt_hbm, kmt_ref), (fs_hbm, fs), (fo_hbm, fo)))
    ]
    for copy in flat:
        copy.start()
    copies = []
    for c in range(rows // chunk):
        part = pl.ds(c * chunk, chunk)
        trio = (
            pltpu.make_async_copy(tr_hbm.at[:, :, part], tr.at[:, :, part], sems.at[c, 0]),
            pltpu.make_async_copy(ve_hbm.at[:, :, part], ve.at[:, :, part], sems.at[c, 1]),
            pltpu.make_async_copy(di_hbm.at[:, part], di.at[:, part], sems.at[c, 2]),
        )
        for copy in trio:
            copy.start()
        copies.append(trio)
    shape = (chunk, cols)
    lane, row = lanes_of(shape), rows_of(shape)
    base = 6 * levels
    first, last = lane == 0, lane == cols - 1
    lean = jnp.where(last, -0.5, 0.5)
    pack = jnp.zeros(shape, jnp.float32)
    for copy in flat:
        copy.wait()
    ready = 0
    for c in range(rows // chunk):
        start = c * chunk
        while ready < min(c + 2, rows // chunk):
            for copy in copies[ready]:
                copy.wait()
            ready += 1
        part = pl.ds(start, chunk)
        kmt = kmt_ref[part, :]
        offset = c * (6 * levels + 16)
        heavy = jnp.where(kmt > 0, 4.0 + fs[part, :], 0.0)
        weight[part, :] = heavy
        mixed = jnp.zeros(shape, jnp.float32)
        carried = jnp.zeros(shape, jnp.float32)

        def row_jump(k, at):
            if at < 0 or at >= rows:
                return jnp.zeros((1, cols), jnp.float32)
            one = pl.ds(at, 1)
            return jnp.where(kmt_ref[one, :] > k, tr[0, k, one, :] - tr[1, k, one, :], 0.0)

        for k in range(levels):
            wet = kmt > k
            values = [jnp.where(wet, tr[t, k, part, :], 0.0) for t in range(2)]
            mixing, u, v = di[k, part, :], ve[0, k, part, :], ve[1, k, part, :]
            edge = jnp.where(wet, mixing + lean * u, 0.0)
            for i, field in enumerate((*values, edge)):
                slot = offset // 2 + i * levels + k
                pack = jnp.where((lane // 2) == slot, roll(field, 2 * slot + 1), pack)
            jump = values[0] - values[1]
            east = jnp.where(last, 0.0, roll(jump, -1))
            west = jnp.where(first, 0.0, roll(jump, 1))
            north = jnp.where(row == chunk - 1, row_jump(k, start + chunk), roll(jump, -1, 0))
            south = jnp.where(row == 0, row_jump(k, start - 1), roll(jump, 1, 0))
            around = (east + west) + (north + south) - 4.0 * jump
            mixed = mixed + jnp.where(wet, jump + mixing * around, 0.0)
            carried = carried + jnp.where(wet, u * (east - west) + v * (north - south), 0.0)
            for ref, at, sign in ((bottom, 0, 0.5), (top, rows - 1, -0.5)):
                if start <= at < start + chunk:
                    here = slice(at - start, at - start + 1)
                    for i, field in enumerate(values):
                        ref[pl.ds(i * levels + k, 1), :] = field[here]
                    ref[pl.ds(2 * levels + k, 1), :] = jnp.where(wet[here], mixing[here] + sign * v[here], 0.0)
        rhs = jnp.where(kmt > 0, fo[part, :] + (mixed - 0.5 * carried) / levels, 0.0)
        rhs_out[part, :] = rhs
        for i, field in enumerate((rhs, heavy)):
            at = offset + base + 8 * i
            pack = jnp.where((lane // 8) == at // 8, roll(field, at + REACH), pack)
    packed[pl.ds(0, chunk), :] = pack
    small = (levels, cols)
    lane_s, row_s = lanes_of(small), rows_of(small)
    corner = jnp.zeros((TILE, cols), jnp.float32)
    row_c = rows_of((TILE, cols))
    for i, ref in enumerate((bottom, top)):
        jump = ref[pl.ds(0, levels), :] - ref[pl.ds(levels, levels), :]
        past = ref[pl.ds(2 * levels, levels), :]
        line = jnp.zeros(small, jnp.float32)
        for start, field in ((0, jump), (8 * levels, past)):
            spread = pltpu.roll(field, (start + REACH) % cols, 1, stride=8, stride_axis=0)
            line = line + jnp.where((lane_s // 8) == start // 8 + row_s, spread, 0.0)
        corner = jnp.where(row_c == i, jnp.sum(line, axis=0, keepdims=True), corner)
    packed[pl.ds(chunk, TILE), :] = corner


def tracers_kernel(tr, ve, di, kmt_ref, own_ref, east_west_a, east_west_b, top, bottom, north_south_a, north_south_b, new_out):
    levels = tr.shape[1]
    rows, cols = kmt_ref.shape
    shape = (rows, cols)
    lane, row = lanes_of(shape), rows_of(shape)
    kmt = kmt_ref[...]
    east, west = sides("bx", east_west_a[pl.ds(0, rows // 2), :], east_west_b[pl.ds(0, rows // 2), :])
    east, west = unfold(east, rows, levels), unfold(west, rows, levels)
    north, south = sides("by", north_south_a[pl.ds(0, 3 * levels), :], north_south_b[pl.ds(0, 3 * levels), :])
    beyond = jnp.where(lane % 2 == 0, roll(east, -1), roll(west, 1))
    mine = unfold(own_ref[pl.ds(0, rows // 2), :], rows, levels)
    ends = (lane == 0) | (lane == cols - 1)
    top_v, bottom_v = top[...], bottom[...]
    added = [mine * roll(beyond, 4 * levels - 2 * levels * t) for t in range(2)]
    above = [top_v[2 * levels :] * north[t * levels : (t + 1) * levels] for t in range(2)]
    below = [bottom_v[2 * levels :] * south[t * levels : (t + 1) * levels] for t in range(2)]
    for k in range(levels):
        wet, own, *around = level_terms(kmt, k, di[k], ve[0, k], ve[1, k])
        around = inside(*around, lane, row)
        for t in range(2):
            value = within(jnp.where(wet, tr[t, k], 0.0), own, *around)
            value = value + jnp.where(ends, roll(added[t], cols - 1 - (4 * levels + 2 * k)), 0.0)
            value = value + jnp.where(row == rows - 1, above[t][k : k + 1], 0.0) + jnp.where(row == 0, below[t][k : k + 1], 0.0)
            new_out[t, k] = value


def is_even(axis):
    return lax.axis_index(axis) % 2 == 0 if lax.axis_size(axis) % 2 == 0 else lax.axis_size(axis) > 0


def sides(axis, got_a, got_b):
    index, even = lax.axis_index(axis), is_even(axis)
    after = jnp.where(even, got_a, got_b)
    before = jnp.where(even, got_b, got_a)
    return jnp.where(index < lax.axis_size(axis) - 1, after, 0.0), jnp.where(index > 0, before, 0.0)


def columns_kernel(got_a, got_b, packed, top, bottom, weight, rhs_in, strip_out, rhs_out, send_a, send_b):
    rows, cols = weight.shape
    levels = top.shape[0] // 3
    east, west = sides("bx", got_a[...], got_b[...])
    shape = (rows, cols)
    lane = lanes_of(shape)
    mine = unfold(packed[pl.ds(0, rows // 2), :], rows, levels)
    e, w = unfold(east, rows, levels), unfold(west, rows, levels)
    beyond = jnp.where(lane % 2 == 0, roll(e, -1), roll(w, 1))
    jump_beyond = roll(beyond, 4 * levels) - roll(beyond, 2 * levels)
    jump_mine = roll(mine, 4 * levels) - roll(mine, 2 * levels)
    here = (lane >= 4 * levels) & (lane < 6 * levels)
    inward = jnp.where(here, mine * jump_beyond, 0.0)
    outward = jnp.where(here, beyond * jump_mine, 0.0)
    both = inward + roll(outward, 2 * levels)
    both = grouped_sum(both, 2, 2 * levels) / levels
    ends = (lane == 0) | (lane == cols - 1)
    rhs = rhs_in[...] + jnp.where(ends, roll(both, cols - 1 - (6 * levels - 2)), 0.0)
    rhs_out[...] = rhs
    base = 6 * levels
    first = roll(both, base + REACH - (8 * levels - 2))
    second = roll(both, base + REACH - 1 - (8 * levels - 1))
    body = jnp.where(lane % 8 < REACH, w, e) + jnp.where(lane == base + REACH, first, 0.0) + jnp.where(lane == base + REACH - 1, second, 0.0)
    strip_out[pl.ds(0, rows), :] = body
    tile = (TILE, cols)
    corner = jnp.where(lanes_of(tile) % 8 < REACH, west[rows // 2 :], east[rows // 2 :])
    strip_out[pl.ds(rows, TILE), :] = corner
    row = rows_of(tile)
    heavy = weight[...]
    n3 = 3 * levels
    above = (
        top[...],
        jnp.where(row < REACH, roll(heavy[rows - TILE :], REACH, 0), rhs[rows - TILE :]),
        jnp.where(row == 0, corner[1:2], body[rows - TILE :]),
    )
    below = (
        bottom[...],
        jnp.where(row < REACH, rhs[:TILE], roll(heavy[:TILE], REACH, 0)),
        jnp.where(row == REACH, corner[:1], body[:TILE]),
    )
    even = is_even("by")
    for ref, one, two in ((send_a, above, below), (send_b, below, above)):
        ref[pl.ds(0, n3), :] = jnp.where(even, one[0], two[0])
        ref[pl.ds(n3, TILE), :] = jnp.where(even, one[1], two[1])
        ref[pl.ds(n3 + TILE, TILE), :] = jnp.where(even, one[2], two[2])


def rows_kernel(got_a, got_b, top, bottom, weight, rhs_in, strip_in, basis, moments):
    rows, cols = weight.shape
    levels = top.shape[0] // 3
    north, south = sides("by", got_a[...], got_b[...])
    n3 = 3 * levels

    def jump(block):
        return block[:levels] - block[levels : 2 * levels]

    def dot(coefficient, value):
        return jnp.sum(coefficient * value, axis=0, keepdims=True) / levels

    top_v, bottom_v = top[...], bottom[...]
    add_top = dot(top_v[2 * levels :], jump(north[:n3]))
    add_bottom = dot(bottom_v[2 * levels :], jump(south[:n3]))
    add_north = dot(north[2 * levels : n3], jump(top_v))
    add_south = dot(south[2 * levels : n3], jump(bottom_v))
    corner = strip_in[pl.ds(rows, TILE), :]
    low, high = corner[:1], corner[1:2]
    c_north, c_south = north[n3 + TILE + REACH : n3 + TILE + REACH + 1], south[n3 + TILE : n3 + TILE + 1]
    half = 8 * levels
    edge = (1, cols)
    lane_1 = lanes_of(edge)

    def cross(coefficient, value):
        product = jnp.where(lane_1 >= half, coefficient * roll(value, half), 0.0)
        summed = grouped_sum(product, 8, 8 * levels) / levels
        return jnp.where((lane_1 // 8) == 6 * levels // 8, roll(summed, 6 * levels - (16 * levels - 8)), 0.0)

    strip_top, strip_bottom = cross(high, c_north), cross(low, c_south)
    strip_north, strip_south = cross(c_north, high), cross(c_south, low)

    extended = (rows + 2 * TILE, cols)
    row = rows_of(extended)
    lane = lanes_of(extended)

    outer = rows_of((TILE, cols))
    flat_n, flat_s = north[n3 : n3 + TILE], south[n3 : n3 + TILE]
    strip_n, strip_s = north[n3 + TILE :], south[n3 + TILE :]

    def extend(own, above, below):
        pieces = [own, jnp.where(outer < REACH, above, 0.0), jnp.where(outer >= TILE - REACH, below, 0.0)]
        return jnp.concatenate(pieces, axis=0)

    def patch(field, at_top, at_bottom, at_north, at_south):
        field = field + jnp.where(row == rows - 1, at_top, 0.0) + jnp.where(row == 0, at_bottom, 0.0)
        return field + jnp.where(row == rows, at_north, 0.0) + jnp.where(row == rows + 2 * TILE - 1, at_south, 0.0)

    rhs_c = patch(extend(rhs_in[...], flat_n, flat_s), add_top, add_bottom, add_north, add_south)
    heavy_c = extend(weight[...], roll(flat_n, REACH, 0), roll(flat_s, REACH, 0))
    strip = extend(strip_in[pl.ds(0, rows), :], strip_n, strip_s)
    strip = patch(strip, strip_top, strip_bottom, strip_north, strip_south)
    near = (lane < REACH) | (lane >= cols - REACH)
    base = 6 * levels
    rhs_s, heavy_s = (jnp.where(near, roll(strip, cols - REACH - base - 8 * i), 0.0) for i in range(2))

    scale = 1.0 / HALFWIDTH
    diag_c, side_c = jnp.where(heavy_c > 0, (heavy_c - CENTER) * scale, 0.0), jnp.where(heavy_c > 0, scale, 0.0)
    diag_s, side_s = jnp.where(heavy_s > 0, (heavy_s - CENTER) * scale, 0.0), jnp.where(heavy_s > 0, scale, 0.0)
    right, left = lane == cols - 1, lane == 0

    def apply(c, s):
        rc, rs, lc, ls = roll(c, -1), roll(s, -1), roll(c, 1), roll(s, 1)
        around_c = jnp.where(right, rs, rc) + jnp.where(left, ls, lc) + roll(c, -1, 0) + roll(c, 1, 0)
        around_s = jnp.where(right, rc, rs) + jnp.where(left, lc, ls) + roll(s, -1, 0) + roll(s, 1, 0)
        return diag_c * c - side_c * around_c, diag_s * s - side_s * around_s

    vectors = [(rhs_c, rhs_s)]
    vectors.append(apply(*vectors[0]))
    for _ in range(ITERS - 1):
        c, s = apply(*vectors[-1])
        vectors.append((2.0 * c - vectors[-2][0], 2.0 * s - vectors[-2][1]))
    inner = [c[:rows] for c, _ in vectors]
    line = jnp.zeros(edge, jnp.float32)
    at = 0
    for i in range(ITERS + 1):
        basis[i] = inner[i]
        for j in range(i, ITERS + 1):
            product = (inner[i] * inner[j]).reshape(rows // TILE, TILE, cols).sum(axis=0)
            whole = jnp.sum(jnp.sum(product, axis=0, keepdims=True), axis=1, keepdims=True)
            line = jnp.where(lane_1 == at, whole, line)
            at += 1
    moments[...] = jnp.broadcast_to(line[None], moments.shape)


def times(coefficients):
    out = [None] * (len(coefficients) + 1)

    def put(at, value):
        out[at] = value if out[at] is None else out[at] + value

    for j, c in enumerate(coefficients):
        put(j, CENTER * c)
        if j == 0:
            put(1, HALFWIDTH * c)
        else:
            put(j + 1, 0.5 * HALFWIDTH * c)
            put(j - 1, 0.5 * HALFWIDTH * c)
    return out


def mix(a, b, factor):
    out = []
    for j in range(max(len(a), len(b))):
        if j >= len(b):
            out.append(a[j])
        elif j >= len(a):
            out.append(factor * b[j])
        else:
            out.append(a[j] + factor * b[j])
    return out


def solve_kernel(got, basis, surface_out, residual_out, flag, results, sems):
    size = ITERS + 1
    line = jnp.sum(got[...], axis=0)
    lane_1 = lanes_of(line.shape)
    gram, at = {}, 0
    for i in range(size):
        for j in range(i, size):
            gram[i, j] = gram[j, i] = jnp.sum(jnp.where(lane_1 == at, line, 0.0), axis=1, keepdims=True)
            at += 1

    def inner(a, b):
        exact = bound = None
        for i, x in enumerate(a):
            for j, y in enumerate(b):
                term = x * y * gram[i, j]
                exact = term if exact is None else exact + term
                bound = jnp.abs(term) if bound is None else bound + jnp.abs(term)
        return exact, bound

    one = jnp.ones_like(gram[0, 0])
    good = one > 0
    residual = [one]
    image = times(residual)
    now, _ = inner(residual, residual)
    product, _ = inner(residual, image)
    alpha = now / product
    direction, along = residual, image
    surface = []
    for step in range(ITERS):
        surface = mix(surface, direction, alpha)
        residual = mix(residual, along, -alpha)
        if step + 1 < ITERS:
            image = times(residual)
            following, bound = inner(residual, residual)
            good = good & (bound <= LIMIT * following)
            product, bound = inner(residual, image)
            good = good & (bound <= LIMIT * product)
            ratio = following / now
            taken = ratio * following / alpha
            good = good & (product + taken <= 0.1 * LIMIT * (product - taken))
            alpha = following / (product - taken)
            direction = mix(residual, direction, ratio)
            along = mix(image, along, ratio)
            now = following
    last, _ = inner(residual, residual)
    good = good & (now <= 0.1 * LIMIT * last)
    vectors = [basis[i] for i in range(size)]
    copies = []
    for at, (ref, combination) in enumerate(((surface_out, surface), (residual_out, residual))):
        total = combination[0] * vectors[0]
        for j in range(1, len(combination)):
            total = total + combination[j] * vectors[j]
        results[at] = total
        copies.append(pltpu.make_async_copy(results.at[at], ref, sems.at[at]))
        copies[at].start()
    flag[0, 0] = jnp.where(good, 1, 0)[0, 0]
    for copy in copies:
        copy.wait()


def linear(axis, index, other):
    row, column = (index, other) if axis == AXES[0] else (other, index)
    return row * lax.axis_size(AXES[1]) + column


def exchange(first, second, axis):
    peers = lax.axis_size(axis)
    if peers % 2:
        up = [(i, i + 1) for i in range(peers - 1)]
        down = [(j, i) for i, j in up]
        return lax.ppermute(second, axis, down), lax.ppermute(first, axis, up)
    pairs_a = [(i, i ^ 1) for i in range(peers)]
    pairs_b = [(i, (i + 1) % peers if i % 2 else (i - 1) % peers) for i in range(peers)]
    other, = [name for name in AXES if name != axis]
    if lax.axis_size(other) % 2 == 0:
        far = []
        for i in range(peers):
            for j in range(lax.axis_size(other)):
                target = (i, j ^ 1) if i in (0, peers - 1) else (pairs_b[i][1], j)
                far.append((linear(axis, i, j), linear(axis, *target)))
        axes, pairs_b = AXES, far
    else:
        axes = axis
    got_a = lax.ppermute(first, axis, pairs_a)
    got_b = lax.ppermute(second, axes, pairs_b)
    return got_a, got_b


def padded_2(value, axes, width):
    for axis, dim in axes:
        peers, length = (lax.axis_size(axis), value.shape[dim])
        up = [(i, (i + 1) % peers) for i in range(peers - 1)]
        down = [(j, i) for i, j in up]
        last = lax.slice_in_dim(value, length - width, length, axis=dim)
        first = lax.slice_in_dim(value, 0, width, axis=dim)
        before = lax.ppermute(last, axis, up)
        after = lax.ppermute(first, axis, down)
        value = jnp.concatenate([before, value, after], axis=dim)
    return value


def step_by_step(rhs, kmt, free_surface):
    ocean = (kmt > 0).astype(jnp.float32)
    weight = ocean * (4.0 + free_surface)

    def operate(field):
        padded = padded_2(field, (("by", 0), ("bx", 1)), 1)
        around = padded[1:-1, 2:] + padded[1:-1, :-2] + padded[2:, 1:-1] + padded[:-2, 1:-1]
        return weight * field - ocean * around

    def pair(a, b):
        return lax.psum(lax.psum((jnp.sum(a * a), jnp.sum(a * b)), "bx"), "by")

    surface, residual = jnp.zeros_like(rhs), rhs
    image = operate(residual)
    now, product = pair(residual, image)
    alpha = now / product
    direction, along = residual, image
    for step in range(ITERS):
        surface = surface + alpha * direction
        residual = residual - alpha * along
        if step + 1 < ITERS:
            image = operate(residual)
            following, product = pair(residual, image)
            ratio = following / now
            alpha = following / (product - ratio * following / alpha)
            direction = residual + ratio * direction
            along = image + ratio * along
            now = following
    return surface, residual


def call(kernel, out_shape, kinds, out_kinds=None, scratch=(), cost=None, resident=True):
    spaces = {"s": pltpu.SMEM, "v": pltpu.VMEM, "h": pltpu.HBM}
    out_kinds = out_kinds or "v" * len(out_shape)
    if resident:
        out_shape = [spaces[k](o.shape, o.dtype) for k, o in zip(out_kinds, out_shape)]
    return pl.pallas_call(
        kernel,
        out_shape=out_shape,
        in_specs=[pl.BlockSpec(memory_space=spaces[k]) for k in kinds],
        out_specs=[pl.BlockSpec(memory_space=spaces[k]) for k in out_kinds],
        scratch_shapes=scratch,
        cost_estimate=cost,
        compiler_params=pltpu.CompilerParams(vmem_limit_bytes=VMEM_GRANT),
    )


def f32(*shape):
    return jax.ShapeDtypeStruct(shape, jnp.float32)


def per_device(*inputs):
    tracers, kmt = inputs[0], inputs[3]
    levels = tracers.shape[1]
    rows, cols = kmt.shape
    everyone = lax.axis_size("by") * lax.axis_size("bx")
    lines = 3 * levels
    packed, top, bottom, rhs, weight, tracers, velocity, diffusivity, kmt = call(
        stencil_kernel,
        [f32(rows // 2 + TILE, cols), f32(lines, cols), f32(lines, cols), f32(rows, cols), f32(rows, cols)]
        + [jax.ShapeDtypeStruct(v.shape, v.dtype) for v in inputs[:4]],
        "h" * 6,
        scratch=[
            pltpu.VMEM((rows, cols), jnp.float32),
            pltpu.VMEM((rows, cols), jnp.float32),
            pltpu.SemaphoreType.DMA((2, 3)),
            pltpu.SemaphoreType.DMA((3,)),
        ],
    )(*[pltpu.with_memory_space_constraint(v, pltpu.HBM) for v in inputs])
    x_a, x_b = exchange(packed, packed, "bx")
    deep = lines + 2 * TILE
    strip, rhs, send_a, send_b = call(
        columns_kernel,
        [f32(rows + TILE, cols), f32(rows, cols), f32(deep, cols), f32(deep, cols)],
        "v" * 7,
    )(x_a, x_b, packed, top, bottom, weight, rhs)
    y_a, y_b = exchange(send_a, send_b, "by")
    basis, moments = call(
        rows_kernel,
        [f32(ITERS + 1, rows, cols), f32(everyone, 1, cols)],
        "v" * 7,
    )(y_a, y_b, top, bottom, weight, rhs, strip)
    got = lax.all_to_all(moments, ("by", "bx"), 0, 0, tiled=True)
    new_tracers, = call(
        tracers_kernel,
        [f32(*tracers.shape)],
        "v" * 11,
        resident=False,
        cost=pl.CostEstimate(flops=30 * tracers.size, bytes_accessed=16 * tracers.size, transcendentals=0),
    )(tracers, velocity, diffusivity, kmt, packed, x_a, x_b, top, bottom, y_a, y_b)
    surface, residual, flag = call(
        solve_kernel,
        [f32(rows, cols), f32(rows, cols), jax.ShapeDtypeStruct((1, 1), jnp.int32)],
        "vv",
        "hhs",
        scratch=[pltpu.VMEM((2, rows, cols), jnp.float32), pltpu.SemaphoreType.DMA((2,))],
    )(got, basis)
    surface, residual = lax.cond(
        flag[0, 0] == 1,
        lambda: (surface, residual),
        lambda: step_by_step(basis[0], inputs[3], inputs[5]),
    )
    return new_tracers, surface, residual


def solution(mesh):
    placed = (
        P(None, None, "by", "bx"),
        P(None, None, "by", "bx"),
        P(None, "by", "bx"),
        P("by", "bx"),
        P("by", "bx"),
        P("by", "bx"),
    )
    return jax.shard_map(
        per_device,
        mesh=mesh,
        in_specs=placed,
        out_specs=(P(None, None, "by", "bx"), P("by", "bx"), P("by", "bx")),
        check_vma=False,
    )
```

profile of v0, /device:TPU:0, one launch (start us, length us, event | category | flops | bytes accessed | tf_op | source)
XLA Modules:
  0.0 29.2 jit_solution(8601497641452435072)
XLA Ops:
  0.6 2.4 %shard_map.85 = (f32[56,128]{1,0:T(8,128)S(1)}, f32[24,128]{1,0:T(8,128)S(1)}, f32[24,128]{1,0:T(8,128)S(1)}, f32[96,128]{1,0:T(8,128)S(1)}, f32[96,128]{1,0:T(8...) custom-call(f32[2,8,96,128]{3,2,1,0:T(8,128)} %tr_hbm.1, ...), custom_call_target="tpu_custom_call" | custom-call | tf_op jit(solution)/shard_map/pallas_call | solution.py:524
  3.0 0.6 %collective-permute-start.16 = (f32[56,128]{1,0:T(8,128)S(1)}, f32[56,128]{1,0:T(8,128)S(1)}, u32[]{:S(2)}, u32[]{:S(2)}) collective-permute-start(f32[56,128]{1,0:T(8,128)S(1)} %get-tuple-element.40.packed.own_ref), channel_id=1, source_target_pairs={{0,1},{1,0},{2,3},{3,2},{4,5},{5,4},{6,7},{7,6},{8,9},{9,8},{10,11... | collective-permute-start | bytes 86024 | tf_op jit(solution)/shard_map/ppermute | solution.py:449
  3.6 2.6 %collective-permute-start.17 = (f32[56,128]{1,0:T(8,128)S(1)}, f32[56,128]{1,0:T(8,128)S(1)}, u32[]{:S(2)}, u32[]{:S(2)}) collective-permute-start(f32[56,128]{1,0:T(8,128)S(1)} %get-tuple-element.40.packed.own_ref), channel_id=1, source_target_pairs={{0,8},{8,0},{16,24},{24,16},{1,2},{9,10},{17,18},{25,26},{2,1},{10... | collective-permute-start | bytes 86024 | tf_op jit(solution)/shard_map/ppermute | solution.py:450
  6.1 0.0 collective-permute-done.16.got_a.east_west_a
  6.1 1.8 %collective-permute-done.17.got_b.east_west_b = f32[56,128]{1,0:T(8,128)S(1)} collective-permute-done((f32[56,128]{1,0:T(8,128)S(1)}, f32[56,128]{1,0:T(8,128)S(1)}, u32[]{:S(2)}, u32[]{:S(2)}) %collective-permute-start.17) | collective-permute-done | bytes 28704 | tf_op jit(solution)/shard_map/ppermute | solution.py:450
  8.0 0.5 %shard_map.86 = (f32[104,128]{1,0:T(8,128)S(1)}, f32[96,128]{1,0:T(8,128)S(1)}, f32[40,128]{1,0:T(8,128)S(1)}, f32[40,128]{1,0:T(8,128)S(1)}) custom-call(f32[56,128]{1,0:T(8,128)S(1)} %collective-permute-done.16.got_a.east_west_a, f32[56,128]{1,0:T(8,128)S(1)} %collective-permute-done.17.got_b.east_west_b, f32[56,128]{1,0:T(8,128)S(1)} %get-tuple-element.40.packed.own_ref, ...), custom_call_target="tpu_custom_call" | custom-call | tf_op jit(solution)/shard_map/pallas_call | solution.py:538
  8.5 2.1 %collective-permute-start.18 = (f32[40,128]{1,0:T(8,128)S(1)}, f32[40,128]{1,0:T(8,128)S(1)}, u32[]{:S(2)}, u32[]{:S(2)}) collective-permute-start(f32[40,128]{1,0:T(8,128)S(1)} %get-tuple-element.45), channel_id=1, source_target_pairs={{0,8},{8,0},{16,24},{24,16},{1,9},{9,1},{17,25},{25,17},{2,10},{10... | collective-permute-start | bytes 61448 | tf_op jit(solution)/shard_map/ppermute | solution.py:449
  10.6 0.0 collective-permute-start.19
  10.6 1.8 %collective-permute-done.18.north_south_a.got_a = f32[40,128]{1,0:T(8,128)S(1)} collective-permute-done((f32[40,128]{1,0:T(8,128)S(1)}, f32[40,128]{1,0:T(8,128)S(1)}, u32[]{:S(2)}, u32[]{:S(2)}) %collective-permute-start.18) | collective-permute-done | bytes 20512 | tf_op jit(solution)/shard_map/ppermute | solution.py:449
  12.4 0.0 collective-permute-done.19.north_south_b.got_b
  12.4 1.5 %shard_map.88 = (f32[5,96,128]{2,1,0:T(8,128)S(1)}, f32[32,1,128]{2,1,0:T(1,128)}) custom-call(f32[40,128]{1,0:T(8,128)S(1)} %collective-permute-done.18.north_south_a.got_a, f32[40,128]{1,0:T(8,128)S(1)} %collective-permute-done.19.north_south_b.got_b, f32[24,128]{1,0:T(8,128)S(1)} %get-tuple-element.41.top, f32[24,128]{1,0:T(8,128)S(1)} %get-tuple-element.42.bottom, ...), custom_call_target="tpu_custom_call" | custom-call | tf_op jit(solution)/shard_map/pallas_call | solution.py:544
  13.9 7.3 %all-to-all-start = ((f32[32,1,128]{2,1,0:T(1,128)}), f32[32,1,128]{2,1,0:T(1,128)S(1)}, u32[]{:S(2)}, u32[]{:S(2)}) async-start(f32[32,1,128]{2,1,0:T(1,128)} %get-tuple-element.49), calls=%async_computation | async-start | bytes 32768 | tf_op jit(solution)/shard_map/all_to_all | solution.py:549
  21.2 1.8 %shard_map.87 = f32[2,8,96,128]{3,2,1,0:T(8,128)} custom-call(f32[2,8,96,128]{3,2,1,0:T(8,128)S(1)} %get-tuple-element.36.tr, f32[2,8,96,128]{3,2,1,0:T(8,128)S(1)} %get-tuple-element.37.ve, f32[8,96,128]{2,1,0:T(8,128)S(1)} %get-tuple-element.38.di, s32[96,128]{1,0:T(8,128)S(1)} %get-tuple-element.39.kmt_ref, ...), custom_call_target="tpu_custom_call" | custom-call | flops 5898240 | bytes 3145728 | tf_op jit(solution)/shard_map/pallas_call | solution.py:550
  23.0 0.0 copy-start
  23.0 0.0 copy-start.1
  23.0 5.3 %all-to-all-done.got = f32[32,1,128]{2,1,0:T(1,128)S(1)} async-done(((f32[32,1,128]{2,1,0:T(1,128)}), f32[32,1,128]{2,1,0:T(1,128)S(1)}, u32[]{:S(2)}, u32[]{:S(2)}) %all-to-all-start) | async-done | bytes 16416 | tf_op jit(solution)/shard_map/all_to_all | solution.py:549
  28.3 0.9 %shard_map.89 = (f32[96,128]{1,0:T(8,128)}, f32[96,128]{1,0:T(8,128)}, s32[1,1]{1,0:T(1,128)S(4)}) custom-call(f32[32,1,128]{2,1,0:T(1,128)S(1)} %all-to-all-done.got, f32[5,96,128]{2,1,0:T(8,128)S(1)} %get-tuple-element.50.basis), custom_call_target="tpu_custom_call" | custom-call | tf_op jit(solution)/shard_map/pallas_call | solution.py:557
  29.2 0.0 copy-done
  29.2 0.0 copy-done.1
  (1 shorter events, 0.0 us)
Async XLA Ops:
  3.0 3.1 %collective-permute-start.16 = (f32[56,128]{1,0:T(8,128)S(1)}, f32[56,128]{1,0:T(8,128)S(1)}, u32[]{:S(2)}, u32[]{:S(2)}) collective-permute-start(f32[56,128]{1,0:T(8,128)S(1)} %get-tuple-element.40.packed.own_ref), channel_id=1, source_target_pairs={{0,1},{1,0},{2,3},{3,2},{4,5},{5,4},{6,7},{7,6},{8,9},{9,8},{10,11... | collective-permute-start | bytes 86024 | tf_op jit(solution)/shard_map/ppermute | solution.py:449
  3.6 4.4 %collective-permute-start.17 = (f32[56,128]{1,0:T(8,128)S(1)}, f32[56,128]{1,0:T(8,128)S(1)}, u32[]{:S(2)}, u32[]{:S(2)}) collective-permute-start(f32[56,128]{1,0:T(8,128)S(1)} %get-tuple-element.40.packed.own_ref), channel_id=1, source_target_pairs={{0,8},{8,0},{16,24},{24,16},{1,2},{9,10},{17,18},{25,26},{2,1},{10... | collective-permute-start | bytes 86024 | tf_op jit(solution)/shard_map/ppermute | solution.py:450
  8.5 3.8 %collective-permute-start.18 = (f32[40,128]{1,0:T(8,128)S(1)}, f32[40,128]{1,0:T(8,128)S(1)}, u32[]{:S(2)}, u32[]{:S(2)}) collective-permute-start(f32[40,128]{1,0:T(8,128)S(1)} %get-tuple-element.45), channel_id=1, source_target_pairs={{0,8},{8,0},{16,24},{24,16},{1,9},{9,1},{17,25},{25,17},{2,10},{10... | collective-permute-start | bytes 61448 | tf_op jit(solution)/shard_map/ppermute | solution.py:449
  10.6 1.8 %collective-permute-start.19 = (f32[40,128]{1,0:T(8,128)S(1)}, f32[40,128]{1,0:T(8,128)S(1)}, u32[]{:S(2)}, u32[]{:S(2)}) collective-permute-start(f32[40,128]{1,0:T(8,128)S(1)} %get-tuple-element.46), channel_id=1, source_target_pairs={{0,1},{1,0},{2,3},{3,2},{4,5},{5,4},{6,7},{7,6},{8,16},{9,17},{10,... | collective-permute-start | bytes 61448 | tf_op jit(solution)/shard_map/ppermute | solution.py:450
  13.9 14.4 %all-to-all-start = ((f32[32,1,128]{2,1,0:T(1,128)}), f32[32,1,128]{2,1,0:T(1,128)S(1)}, u32[]{:S(2)}, u32[]{:S(2)}) async-start(f32[32,1,128]{2,1,0:T(1,128)} %get-tuple-element.49), calls=%async_computation | async-start | bytes 32768 | tf_op jit(solution)/shard_map/all_to_all | solution.py:549
  23.0 6.2 %copy-start = (f32[96,128]{1,0:T(8,128)S(1)}, f32[96,128]{1,0:T(8,128)}, u32[]{:S(2)}) copy-start(f32[96,128]{1,0:T(8,128)} %fs_hbm.1) | copy-start | bytes 147460
  23.0 6.2 %copy-start.1 = (s32[96,128]{1,0:T(8,128)S(1)}, s32[96,128]{1,0:T(8,128)}, u32[]{:S(2)}) copy-start(s32[96,128]{1,0:T(8,128)} %kmt_hbm.1) | copy-start | bytes 147460
where the time goes:
time: 29.4 us; the launch traced here: 29.2 us
  starting transfers between devices  12.5 us (43%)
  waiting for transfers between devices  8.92 us (30%)
  Pallas kernels  7.13 us (24%)
  between operations  0.69 us (2%)
    all_to_all x1, starting transfers between devices, per_device(): got = lax.all_to_all(moments, ('by', 'bx'), 0, 0, tiled=True)  7.26 us
    all_to_all x1, waiting for transfers between devices, per_device(): got = lax.all_to_all(moments, ('by', 'bx'), 0, 0, tiled=True)  5.31 us
    ppermute x2, starting transfers between devices, exchange(): got_a = lax.ppermute(first, axis, pairs_a)  2.64 us
    ppermute x2, starting transfers between devices, exchange(): got_b = lax.ppermute(second, axes, pairs_b)  2.55 us
    pallas_call x1, Pallas kernels, per_device(): call(stencil_kernel, [f32(rows // 2 + TILE, cols), f32(lines, cols), f32(...  2.37 us
    ppermute x2, waiting for transfers between devices, exchange(): got_b = lax.ppermute(second, axes, pairs_b)  1.85 us
    pallas_call x1, Pallas kernels, per_device(): call(tracers_kernel, [f32(*tracers.shape)], 'v' * 11, resident=False, cos...  1.79 us
    ppermute x2, waiting for transfers between devices, exchange(): got_a = lax.ppermute(first, axis, pairs_a)  1.76 us
  transfers between devices with their start and end apart: 5, of which 3 were waited for; matrix products, arithmetic and copies ran while one was open for 0% of the time, Pallas kernels for 6%

commit v1 on v0

--- a/solution.py
+++ b/solution.py
@@ -13,6 +13,7 @@
 CENTER = 5.0
 HALFWIDTH = 4.0
 VMEM_GRANT = 12 << 20
+GROUPS = 2
 LIMIT = 1000.0
 
 
@@ -83,17 +84,20 @@
     ]
     for copy in flat:
         copy.start()
+    span = levels // GROUPS
     copies = []
-    for c in range(rows // chunk):
-        part = pl.ds(c * chunk, chunk)
-        trio = (
-            pltpu.make_async_copy(tr_hbm.at[:, :, part], tr.at[:, :, part], sems.at[c, 0]),
-            pltpu.make_async_copy(ve_hbm.at[:, :, part], ve.at[:, :, part], sems.at[c, 1]),
-            pltpu.make_async_copy(di_hbm.at[:, part], di.at[:, part], sems.at[c, 2]),
-        )
-        for copy in trio:
-            copy.start()
-        copies.append(trio)
+    for c, (begin, length) in enumerate(((0, chunk + TILE), (chunk + TILE, chunk - TILE))):
+        part = pl.ds(begin, length)
+        for g in range(GROUPS):
+            deep = pl.ds(g * span, span)
+            trio = (
+                pltpu.make_async_copy(tr_hbm.at[:, deep, part], tr.at[:, deep, part], sems.at[c, g, 0]),
+                pltpu.make_async_copy(ve_hbm.at[:, deep, part], ve.at[:, deep, part], sems.at[c, g, 1]),
+                pltpu.make_async_copy(di_hbm.at[deep, part], di.at[deep, part], sems.at[c, g, 2]),
+            )
+            for copy in trio:
+                copy.start()
+            copies.append(trio)
     shape = (chunk, cols)
     lane, row = lanes_of(shape), rows_of(shape)
     base = 6 * levels
@@ -102,13 +106,8 @@
     pack = jnp.zeros(shape, jnp.float32)
     for copy in flat:
         copy.wait()
-    ready = 0
     for c in range(rows // chunk):
         start = c * chunk
-        while ready < min(c + 2, rows // chunk):
-            for copy in copies[ready]:
-                copy.wait()
-            ready += 1
         part = pl.ds(start, chunk)
         kmt = kmt_ref[part, :]
         offset = c * (6 * levels + 16)
@@ -124,6 +123,9 @@
             return jnp.where(kmt_ref[one, :] > k, tr[0, k, one, :] - tr[1, k, one, :], 0.0)
 
         for k in range(levels):
+            if k % span == 0:
+                for copy in copies[c * GROUPS + k // span]:
+                    copy.wait()
             wet = kmt > k
             values = [jnp.where(wet, tr[t, k, part, :], 0.0) for t in range(2)]
             mixing, u, v = di[k, part, :], ve[0, k, part, :], ve[1, k, part, :]
@@ -203,14 +205,9 @@
     return jnp.where(index < lax.axis_size(axis) - 1, after, 0.0), jnp.where(index > 0, before, 0.0)
 
 
-def columns_kernel(got_a, got_b, packed, top, bottom, weight, rhs_in, strip_out, rhs_out, send_a, send_b):
-    rows, cols = weight.shape
-    levels = top.shape[0] // 3
-    east, west = sides("bx", got_a[...], got_b[...])
-    shape = (rows, cols)
-    lane = lanes_of(shape)
-    mine = unfold(packed[pl.ds(0, rows // 2), :], rows, levels)
-    e, w = unfold(east, rows, levels), unfold(west, rows, levels)
+def complete(mine, e, w, rhs, levels):
+    cols = mine.shape[1]
+    lane = lanes_of(mine.shape)
     beyond = jnp.where(lane % 2 == 0, roll(e, -1), roll(w, 1))
     jump_beyond = roll(beyond, 4 * levels) - roll(beyond, 2 * levels)
     jump_mine = roll(mine, 4 * levels) - roll(mine, 2 * levels)
@@ -220,28 +217,41 @@
     both = inward + roll(outward, 2 * levels)
     both = grouped_sum(both, 2, 2 * levels) / levels
     ends = (lane == 0) | (lane == cols - 1)
-    rhs = rhs_in[...] + jnp.where(ends, roll(both, cols - 1 - (6 * levels - 2)), 0.0)
-    rhs_out[...] = rhs
+    rhs = rhs + jnp.where(ends, roll(both, cols - 1 - (6 * levels - 2)), 0.0)
     base = 6 * levels
     first = roll(both, base + REACH - (8 * levels - 2))
     second = roll(both, base + REACH - 1 - (8 * levels - 1))
-    body = jnp.where(lane % 8 < REACH, w, e) + jnp.where(lane == base + REACH, first, 0.0) + jnp.where(lane == base + REACH - 1, second, 0.0)
-    strip_out[pl.ds(0, rows), :] = body
+    strip = jnp.where(lane % 8 < REACH, w, e)
+    strip = strip + jnp.where(lane == base + REACH, first, 0.0) + jnp.where(lane == base + REACH - 1, second, 0.0)
+    return rhs, strip
+
+
+def ends_kernel(got_a, got_b, packed, top, bottom, weight, rhs_in, send_a, send_b, corner_out):
+    rows, cols = weight.shape
+    levels = top.shape[0] // 3
+    east, west = sides("bx", got_a[...], got_b[...])
+
+    def outer_rows(block):
+        last = block[rows // 2 - TILE : rows // 2]
+        return jnp.concatenate([block[:TILE], roll(last, -(6 * levels + 16))], axis=0)
+
+    rhs = jnp.concatenate([rhs_in[pl.ds(0, TILE), :], rhs_in[pl.ds(rows - TILE, TILE), :]], axis=0)
+    rhs, strip = complete(outer_rows(packed[...]), outer_rows(east), outer_rows(west), rhs, levels)
     tile = (TILE, cols)
     corner = jnp.where(lanes_of(tile) % 8 < REACH, west[rows // 2 :], east[rows // 2 :])
-    strip_out[pl.ds(rows, TILE), :] = corner
+    corner_out[...] = corner
     row = rows_of(tile)
-    heavy = weight[...]
+    first, last = weight[pl.ds(0, TILE), :], weight[pl.ds(rows - TILE, TILE), :]
     n3 = 3 * levels
     above = (
         top[...],
-        jnp.where(row < REACH, roll(heavy[rows - TILE :], REACH, 0), rhs[rows - TILE :]),
-        jnp.where(row == 0, corner[1:2], body[rows - TILE :]),
+        jnp.where(row < REACH, roll(last, REACH, 0), rhs[TILE:]),
+        jnp.where(row == 0, corner[1:2], strip[TILE:]),
     )
     below = (
         bottom[...],
-        jnp.where(row < REACH, rhs[:TILE], roll(heavy[:TILE], REACH, 0)),
-        jnp.where(row == REACH, corner[:1], body[:TILE]),
+        jnp.where(row < REACH, rhs[:TILE], roll(first, REACH, 0)),
+        jnp.where(row == REACH, corner[:1], strip[:TILE]),
     )
     even = is_even("by")
     for ref, one, two in ((send_a, above, below), (send_b, below, above)):
@@ -250,7 +260,60 @@
         ref[pl.ds(n3 + TILE, TILE), :] = jnp.where(even, one[2], two[2])
 
 
-def rows_kernel(got_a, got_b, top, bottom, weight, rhs_in, strip_in, basis, moments):
+def krylov(rhs_c, heavy_c, strip, heavy_strip):
+    lane = lanes_of(rhs_c.shape)
+    cols = rhs_c.shape[1]
+    near = (lane < REACH) | (lane >= cols - REACH)
+    rhs_s, heavy_s = jnp.where(near, strip, 0.0), jnp.where(near, heavy_strip, 0.0)
+    scale = 1.0 / HALFWIDTH
+    diag_c, side_c = jnp.where(heavy_c > 0, (heavy_c - CENTER) * scale, 0.0), jnp.where(heavy_c > 0, scale, 0.0)
+    diag_s, side_s = jnp.where(heavy_s > 0, (heavy_s - CENTER) * scale, 0.0), jnp.where(heavy_s > 0, scale, 0.0)
+    right, left = lane == cols - 1, lane == 0
+
+    def apply(c, s):
+        rc, rs, lc, ls = roll(c, -1), roll(s, -1), roll(c, 1), roll(s, 1)
+        around_c = jnp.where(right, rs, rc) + jnp.where(left, ls, lc) + roll(c, -1, 0) + roll(c, 1, 0)
+        around_s = jnp.where(right, rc, rs) + jnp.where(left, lc, ls) + roll(s, -1, 0) + roll(s, 1, 0)
+        return diag_c * c - side_c * around_c, diag_s * s - side_s * around_s
+
+    vectors = [(rhs_c, rhs_s)]
+    vectors.append(apply(*vectors[0]))
+    for _ in range(ITERS - 1):
+        c, s = apply(*vectors[-1])
+        vectors.append((2.0 * c - vectors[-2][0], 2.0 * s - vectors[-2][1]))
+    return [c for c, _ in vectors]
+
+
+def products(vectors):
+    cols = vectors[0].shape[1]
+    return [
+        (vectors[i] * vectors[j]).reshape(-1, TILE, cols).sum(axis=0)
+        for i in range(len(vectors))
+        for j in range(i, len(vectors))
+    ]
+
+
+def spread(strip, levels):
+    at = strip.shape[1] - REACH - 6 * levels
+    return roll(strip, at), roll(strip, at - 8)
+
+
+def middle_kernel(got_a, got_b, packed, top, weight, rhs_in, rhs_out, strip_out, basis, sums):
+    rows, _ = weight.shape
+    levels = top.shape[0] // 3
+    east, west = sides("bx", got_a[pl.ds(0, rows // 2), :], got_b[pl.ds(0, rows // 2), :])
+    mine = packed[pl.ds(0, rows // 2), :]
+    rhs, strip = complete(*(unfold(v, rows, levels) for v in (mine, east, west)), rhs_in[...], levels)
+    rhs_out[...] = rhs
+    strip_out[...] = strip
+    vectors = [v[TILE : rows - TILE] for v in krylov(rhs, weight[...], *spread(strip, levels))]
+    for i, v in enumerate(vectors):
+        basis[i] = v
+    for i, v in enumerate(products(vectors)):
+        sums[i] = v
+
+
+def rows_kernel(got_a, got_b, top, bottom, weight, rhs_in, strip_in, corner_in, sums, basis, moments):
     rows, cols = weight.shape
     levels = top.shape[0] // 3
     north, south = sides("by", got_a[...], got_b[...])
@@ -267,7 +330,7 @@
     add_bottom = dot(bottom_v[2 * levels :], jump(south[:n3]))
     add_north = dot(north[2 * levels : n3], jump(top_v))
     add_south = dot(south[2 * levels : n3], jump(bottom_v))
-    corner = strip_in[pl.ds(rows, TILE), :]
+    corner = corner_in[...]
     low, high = corner[:1], corner[1:2]
     c_north, c_south = north[n3 + TILE + REACH : n3 + TILE + REACH + 1], south[n3 + TILE : n3 + TILE + 1]
     half = 8 * levels
@@ -281,57 +344,32 @@
 
     strip_top, strip_bottom = cross(high, c_north), cross(low, c_south)
     strip_north, strip_south = cross(c_north, high), cross(c_south, low)
-
-    extended = (rows + 2 * TILE, cols)
-    row = rows_of(extended)
-    lane = lanes_of(extended)
-
     outer = rows_of((TILE, cols))
     flat_n, flat_s = north[n3 : n3 + TILE], south[n3 : n3 + TILE]
-    strip_n, strip_s = north[n3 + TILE :], south[n3 + TILE :]
-
-    def extend(own, above, below):
-        pieces = [own, jnp.where(outer < REACH, above, 0.0), jnp.where(outer >= TILE - REACH, below, 0.0)]
+
+    def bands(ref, below, above):
+        pieces = [jnp.where(outer >= TILE - REACH, below, 0.0), ref[pl.ds(0, 2 * TILE), :]]
+        pieces += [ref[pl.ds(rows - 2 * TILE, 2 * TILE), :], jnp.where(outer < REACH, above, 0.0)]
         return jnp.concatenate(pieces, axis=0)
 
-    def patch(field, at_top, at_bottom, at_north, at_south):
-        field = field + jnp.where(row == rows - 1, at_top, 0.0) + jnp.where(row == 0, at_bottom, 0.0)
-        return field + jnp.where(row == rows, at_north, 0.0) + jnp.where(row == rows + 2 * TILE - 1, at_south, 0.0)
-
-    rhs_c = patch(extend(rhs_in[...], flat_n, flat_s), add_top, add_bottom, add_north, add_south)
-    heavy_c = extend(weight[...], roll(flat_n, REACH, 0), roll(flat_s, REACH, 0))
-    strip = extend(strip_in[pl.ds(0, rows), :], strip_n, strip_s)
-    strip = patch(strip, strip_top, strip_bottom, strip_north, strip_south)
-    near = (lane < REACH) | (lane >= cols - REACH)
-    base = 6 * levels
-    rhs_s, heavy_s = (jnp.where(near, roll(strip, cols - REACH - base - 8 * i), 0.0) for i in range(2))
-
-    scale = 1.0 / HALFWIDTH
-    diag_c, side_c = jnp.where(heavy_c > 0, (heavy_c - CENTER) * scale, 0.0), jnp.where(heavy_c > 0, scale, 0.0)
-    diag_s, side_s = jnp.where(heavy_s > 0, (heavy_s - CENTER) * scale, 0.0), jnp.where(heavy_s > 0, scale, 0.0)
-    right, left = lane == cols - 1, lane == 0
-
-    def apply(c, s):
-        rc, rs, lc, ls = roll(c, -1), roll(s, -1), roll(c, 1), roll(s, 1)
-        around_c = jnp.where(right, rs, rc) + jnp.where(left, ls, lc) + roll(c, -1, 0) + roll(c, 1, 0)
-        around_s = jnp.where(right, rc, rs) + jnp.where(left, lc, ls) + roll(s, -1, 0) + roll(s, 1, 0)
-        return diag_c * c - side_c * around_c, diag_s * s - side_s * around_s
-
-    vectors = [(rhs_c, rhs_s)]
-    vectors.append(apply(*vectors[0]))
-    for _ in range(ITERS - 1):
-        c, s = apply(*vectors[-1])
-        vectors.append((2.0 * c - vectors[-2][0], 2.0 * s - vectors[-2][1]))
-    inner = [c[:rows] for c, _ in vectors]
+    row = rows_of((6 * TILE, cols))
+
+    def patch(field, at_south, at_bottom, at_top, at_north):
+        field = field + jnp.where(row == TILE - 1, at_south, 0.0) + jnp.where(row == TILE, at_bottom, 0.0)
+        return field + jnp.where(row == 5 * TILE - 1, at_top, 0.0) + jnp.where(row == 5 * TILE, at_north, 0.0)
+
+    rhs_c = patch(bands(rhs_in, flat_s, flat_n), add_south, add_bottom, add_top, add_north)
+    heavy_c = bands(weight, roll(flat_s, REACH, 0), roll(flat_n, REACH, 0))
+    strip = bands(strip_in, south[n3 + TILE :], north[n3 + TILE :])
+    strip = patch(strip, strip_south, strip_bottom, strip_top, strip_north)
+    vectors = krylov(rhs_c, heavy_c, *spread(strip, levels))
+    vectors = [jnp.concatenate([v[TILE : 2 * TILE], v[4 * TILE : 5 * TILE]], axis=0) for v in vectors]
     line = jnp.zeros(edge, jnp.float32)
-    at = 0
-    for i in range(ITERS + 1):
-        basis[i] = inner[i]
-        for j in range(i, ITERS + 1):
-            product = (inner[i] * inner[j]).reshape(rows // TILE, TILE, cols).sum(axis=0)
-            whole = jnp.sum(jnp.sum(product, axis=0, keepdims=True), axis=1, keepdims=True)
-            line = jnp.where(lane_1 == at, whole, line)
-            at += 1
+    for i, v in enumerate(vectors):
+        basis[i] = v
+    for i, v in enumerate(products(vectors)):
+        whole = jnp.sum(jnp.sum(v + sums[i], axis=0, keepdims=True), axis=1, keepdims=True)
+        line = jnp.where(lane_1 == i, whole, line)
     moments[...] = jnp.broadcast_to(line[None], moments.shape)
 
 
@@ -363,7 +401,7 @@
     return out
 
 
-def solve_kernel(got, basis, surface_out, residual_out, flag, results, sems):
+def solve_kernel(got, middle, outer, surface_out, residual_out, flag, results, sems):
     size = ITERS + 1
     line = jnp.sum(got[...], axis=0)
     lane_1 = lanes_of(line.shape)
@@ -409,13 +447,18 @@
             now = following
     last, _ = inner(residual, residual)
     good = good & (now <= 0.1 * LIMIT * last)
-    vectors = [basis[i] for i in range(size)]
+    rows = surface_out.shape[0]
     copies = []
     for at, (ref, combination) in enumerate(((surface_out, surface), (residual_out, residual))):
-        total = combination[0] * vectors[0]
-        for j in range(1, len(combination)):
-            total = total + combination[j] * vectors[j]
-        results[at] = total
+        for part, first, last in ((middle, TILE, rows - TILE), (outer, 0, 2 * TILE)):
+            total = combination[0] * part[0]
+            for j in range(1, len(combination)):
+                total = total + combination[j] * part[j]
+            if part is middle:
+                results[at, pl.ds(first, last - first), :] = total
+            else:
+                results[at, pl.ds(0, TILE), :] = total[:TILE]
+                results[at, pl.ds(rows - TILE, TILE), :] = total[TILE:]
         copies.append(pltpu.make_async_copy(results.at[at], ref, sems.at[at]))
         copies[at].start()
     flag[0, 0] = jnp.where(good, 1, 0)[0, 0]
@@ -529,23 +572,31 @@
         scratch=[
             pltpu.VMEM((rows, cols), jnp.float32),
             pltpu.VMEM((rows, cols), jnp.float32),
-            pltpu.SemaphoreType.DMA((2, 3)),
+            pltpu.SemaphoreType.DMA((2, GROUPS, 3)),
             pltpu.SemaphoreType.DMA((3,)),
         ],
     )(*[pltpu.with_memory_space_constraint(v, pltpu.HBM) for v in inputs])
     x_a, x_b = exchange(packed, packed, "bx")
     deep = lines + 2 * TILE
-    strip, rhs, send_a, send_b = call(
-        columns_kernel,
-        [f32(rows + TILE, cols), f32(rows, cols), f32(deep, cols), f32(deep, cols)],
+    send_a, send_b, corner = call(
+        ends_kernel,
+        [f32(deep, cols), f32(deep, cols), f32(TILE, cols)],
         "v" * 7,
     )(x_a, x_b, packed, top, bottom, weight, rhs)
     y_a, y_b = exchange(send_a, send_b, "by")
-    basis, moments = call(
+    size = ITERS + 1
+    pairs = size * (size + 1) // 2
+    rhs, strip, middle, sums = call(
+        middle_kernel,
+        [f32(rows, cols), f32(rows, cols), f32(size, rows - 2 * TILE, cols), f32(pairs, TILE, cols)],
+        "v" * 6,
+        cost=pl.CostEstimate(flops=200 * rows * cols, bytes_accessed=20 * rows * cols, transcendentals=0),
+    )(x_a, x_b, packed, top, weight, rhs)
+    outer, moments = call(
         rows_kernel,
-        [f32(ITERS + 1, rows, cols), f32(everyone, 1, cols)],
-        "v" * 7,
-    )(y_a, y_b, top, bottom, weight, rhs, strip)
+        [f32(size, 2 * TILE, cols), f32(everyone, 1, cols)],
+        "v" * 9,
+    )(y_a, y_b, top, bottom, weight, rhs, strip, corner, sums)
     got = lax.all_to_all(moments, ("by", "bx"), 0, 0, tiled=True)
     new_tracers, = call(
         tracers_kernel,
@@ -557,14 +608,14 @@
     surface, residual, flag = call(
         solve_kernel,
         [f32(rows, cols), f32(rows, cols), jax.ShapeDtypeStruct((1, 1), jnp.int32)],
-        "vv",
+        "vvv",
         "hhs",
         scratch=[pltpu.VMEM((2, rows, cols), jnp.float32), pltpu.SemaphoreType.DMA((2,))],
-    )(got, basis)
+    )(got, middle, outer)
     surface, residual = lax.cond(
         flag[0, 0] == 1,
         lambda: (surface, residual),
-        lambda: step_by_step(basis[0], inputs[3], inputs[5]),
+        lambda: step_by_step(jnp.concatenate([outer[0, :TILE], middle[0], outer[0, TILE:]]), inputs[3], inputs[5]),
     )
     return new_tracers, surface, residual
 

time: 29.4 us -> 29.1 us (0.990)
  waiting for transfers between devices: 8.92 us -> 7.93 us
  Pallas kernels: 7.13 us -> 7.87 us
    ppermute x2, waiting for transfers between devices: 1.76 us -> 0.78 us  [exchange(): got_a = lax.ppermute(first, axis, pairs_a)]
    pallas_call x2 -> x3, Pallas kernels: 2.08 us -> 2.92 us  [the longest x1 1.46 us: per_device(): call(rows_kernel, [f32(size, 2 * TILE, cols), f32(everyone, 1, cols)], 'v...]
  transfers between devices with their start and end apart: 5 -> 5, of which waited for: 3 -> 3; matrix products, arithmetic and copies ran while one was open for 0% -> 0% of each run, Pallas kernels for 6% -> 10%
where the time goes in v1:
time: 29.1 us; the launch traced here: 28.9 us
  starting transfers between devices  12.4 us (43%)
  waiting for transfers between devices  7.93 us (27%)
  Pallas kernels  7.87 us (27%)
  between operations  0.69 us (2%)
    all_to_all x1, starting transfers between devices, per_device(): got = lax.all_to_all(moments, ('by', 'bx'), 0, 0, tiled=True)  7.26 us
    all_to_all x1, waiting for transfers between devices, per_device(): got = lax.all_to_all(moments, ('by', 'bx'), 0, 0, tiled=True)  5.3 us
    ppermute x2, starting transfers between devices, exchange(): got_a = lax.ppermute(first, axis, pairs_a)  2.6 us
    ppermute x2, starting transfers between devices, exchange(): got_b = lax.ppermute(second, axes, pairs_b)  2.55 us
    pallas_call x1, Pallas kernels, per_device(): call(stencil_kernel, [f32(rows // 2 + TILE, cols), f32(lines, cols), f32(...  2.27 us
    ppermute x2, waiting for transfers between devices, exchange(): got_b = lax.ppermute(second, axes, pairs_b)  1.85 us
    pallas_call x1, Pallas kernels, per_device(): call(tracers_kernel, [f32(*tracers.shape)], 'v' * 11, resident=False, cos...  1.79 us
    pallas_call x1, Pallas kernels, per_device(): call(rows_kernel, [f32(size, 2 * TILE, cols), f32(everyone, 1, cols)], 'v...  1.46 us
  transfers between devices with their start and end apart: 5, of which 3 were waited for; matrix products, arithmetic and copies ran while one was open for 0% of the time, Pallas kernels for 10%

profile of v1, /device:TPU:0, one launch (start us, length us, event | category | flops | bytes accessed | tf_op | source)
XLA Modules:
  0.0 28.9 jit_solution(17660142783465271055)
XLA Ops:
  0.6 2.3 %shard_map.85 = (f32[56,128]{1,0:T(8,128)S(1)}, f32[24,128]{1,0:T(8,128)S(1)}, f32[24,128]{1,0:T(8,128)S(1)}, f32[96,128]{1,0:T(8,128)S(1)}, f32[96,128]{1,0:T(8...) custom-call(f32[2,8,96,128]{3,2,1,0:T(8,128)} %tr_hbm.1, ...), custom_call_target="tpu_custom_call" | custom-call | tf_op jit(solution)/shard_map/pallas_call | solution.py:567
  2.9 0.6 %collective-permute-start.16 = (f32[56,128]{1,0:T(8,128)S(1)}, f32[56,128]{1,0:T(8,128)S(1)}, u32[]{:S(2)}, u32[]{:S(2)}) collective-permute-start(f32[56,128]{1,0:T(8,128)S(1)} %get-tuple-element.46.packed.own_ref), channel_id=1, source_target_pairs={{0,1},{1,0},{2,3},{3,2},{4,5},{5,4},{6,7},{7,6},{8,9},{9,8},{10,11... | collective-permute-start | bytes 86024 | tf_op jit(solution)/shard_map/ppermute | solution.py:492
  3.5 2.6 %collective-permute-start.17 = (f32[56,128]{1,0:T(8,128)S(1)}, f32[56,128]{1,0:T(8,128)S(1)}, u32[]{:S(2)}, u32[]{:S(2)}) collective-permute-start(f32[56,128]{1,0:T(8,128)S(1)} %get-tuple-element.46.packed.own_ref), channel_id=1, source_target_pairs={{0,8},{8,0},{16,24},{24,16},{1,2},{9,10},{17,18},{25,26},{2,1},{10... | collective-permute-start | bytes 86024 | tf_op jit(solution)/shard_map/ppermute | solution.py:493
  6.0 0.0 collective-permute-done.16.got_a.east_west_a
  6.0 1.8 %collective-permute-done.17.got_b.east_west_b = f32[56,128]{1,0:T(8,128)S(1)} collective-permute-done((f32[56,128]{1,0:T(8,128)S(1)}, f32[56,128]{1,0:T(8,128)S(1)}, u32[]{:S(2)}, u32[]{:S(2)}) %collective-permute-start.17) | collective-permute-done | bytes 28704 | tf_op jit(solution)/shard_map/ppermute | solution.py:493
  7.9 0.5 %shard_map.86 = (f32[40,128]{1,0:T(8,128)S(1)}, f32[40,128]{1,0:T(8,128)S(1)}, f32[8,128]{1,0:T(8,128)S(1)}) custom-call(f32[56,128]{1,0:T(8,128)S(1)} %collective-permute-done.16.got_a.east_west_a, f32[56,128]{1,0:T(8,128)S(1)} %collective-permute-done.17.got_b.east_west_b, f32[56,128]{1,0:T(8,128)S(1)} %get-tuple-element.46.packed.own_ref, ...), custom_call_target="tpu_custom_call" | custom-call | tf_op jit(solution)/shard_map/pallas_call | solution.py:581
  8.4 2.0 %collective-permute-start.18 = (f32[40,128]{1,0:T(8,128)S(1)}, f32[40,128]{1,0:T(8,128)S(1)}, u32[]{:S(2)}, u32[]{:S(2)}) collective-permute-start(f32[40,128]{1,0:T(8,128)S(1)} %get-tuple-element.51), channel_id=1, source_target_pairs={{0,8},{8,0},{16,24},{24,16},{1,9},{9,1},{17,25},{25,17},{2,10},{10... | collective-permute-start | bytes 61448 | tf_op jit(solution)/shard_map/ppermute | solution.py:492
  10.4 0.0 collective-permute-start.19
  10.4 1.0 %shard_map.88 = (f32[96,128]{1,0:T(8,128)S(1)}, f32[96,128]{1,0:T(8,128)S(1)}, f32[5,80,128]{2,1,0:T(8,128)S(1)}, f32[15,8,128]{2,1,0:T(8,128)S(1)}) custom-call(f32[56,128]{1,0:T(8,128)S(1)} %collective-permute-done.16.got_a.east_west_a, f32[56,128]{1,0:T(8,128)S(1)} %collective-permute-done.17.got_b.east_west_b, ...), custom_call_target="tpu_custom_call" | custom-call | flops 2457600 | bytes 245760 | tf_op jit(solution)/shard_map/pallas_call | solution.py:589
  11.4 0.8 %collective-permute-done.18.north_south_a.got_a = f32[40,128]{1,0:T(8,128)S(1)} collective-permute-done((f32[40,128]{1,0:T(8,128)S(1)}, f32[40,128]{1,0:T(8,128)S(1)}, u32[]{:S(2)}, u32[]{:S(2)}) %collective-permute-start.18) | collective-permute-done | bytes 20512 | tf_op jit(solution)/shard_map/ppermute | solution.py:492
  12.2 0.0 collective-permute-done.19.north_south_b.got_b
  12.2 1.5 %shard_map.89 = (f32[5,16,128]{2,1,0:T(8,128)S(1)}, f32[32,1,128]{2,1,0:T(1,128)}) custom-call(f32[40,128]{1,0:T(8,128)S(1)} %collective-permute-done.18.north_south_a.got_a, f32[40,128]{1,0:T(8,128)S(1)} %collective-permute-done.19.north_south_b.got_b, f32[24,128]{1,0:T(8,128)S(1)} %get-tuple-element.47.top, f32[24,128]{1,0:T(8,128)S(1)} %get-tuple-element.48.bottom, ...), custom_call_target="tpu_custom_call" | custom-call | tf_op jit(solution)/shard_map/pallas_call | solution.py:595
  13.6 7.3 %all-to-all-start = ((f32[32,1,128]{2,1,0:T(1,128)}), f32[32,1,128]{2,1,0:T(1,128)S(1)}, u32[]{:S(2)}, u32[]{:S(2)}) async-start(f32[32,1,128]{2,1,0:T(1,128)} %get-tuple-element.57), calls=%async_computation | async-start | bytes 32768 | tf_op jit(solution)/shard_map/all_to_all | solution.py:600
  20.9 1.8 %shard_map.87 = f32[2,8,96,128]{3,2,1,0:T(8,128)} custom-call(f32[2,8,96,128]{3,2,1,0:T(8,128)S(1)} %get-tuple-element.42.tr, f32[2,8,96,128]{3,2,1,0:T(8,128)S(1)} %get-tuple-element.43.ve, f32[8,96,128]{2,1,0:T(8,128)S(1)} %get-tuple-element.44.di, s32[96,128]{1,0:T(8,128)S(1)} %get-tuple-element.45.kmt_ref, ...), custom_call_target="tpu_custom_call" | custom-call | flops 5898240 | bytes 3145728 | tf_op jit(solution)/shard_map/pallas_call | solution.py:601
  22.7 0.0 copy-start
  22.7 0.0 copy-start.1
  22.7 5.3 %all-to-all-done.got = f32[32,1,128]{2,1,0:T(1,128)S(1)} async-done(((f32[32,1,128]{2,1,0:T(1,128)}), f32[32,1,128]{2,1,0:T(1,128)S(1)}, u32[]{:S(2)}, u32[]{:S(2)}) %all-to-all-start) | async-done | bytes 16416 | tf_op jit(solution)/shard_map/all_to_all | solution.py:600
  28.0 0.9 %shard_map.90 = (f32[96,128]{1,0:T(8,128)}, f32[96,128]{1,0:T(8,128)}, s32[1,1]{1,0:T(1,128)S(4)}) custom-call(f32[32,1,128]{2,1,0:T(1,128)S(1)} %all-to-all-done.got, f32[5,80,128]{2,1,0:T(8,128)S(1)} %get-tuple-element.58.middle, f32[5,16,128]{2,1,0:T(8,128)S(1)} %get-tuple-element.59.outer), custom_call_target="tpu_custom_call" | custom-call | tf_op jit(solution)/shard_map/pallas_call | solution.py:608
  28.9 0.0 copy-done
  28.9 0.0 copy-done.1
  (1 shorter events, 0.0 us)
Async XLA Ops:
  2.9 3.1 %collective-permute-start.16 = (f32[56,128]{1,0:T(8,128)S(1)}, f32[56,128]{1,0:T(8,128)S(1)}, u32[]{:S(2)}, u32[]{:S(2)}) collective-permute-start(f32[56,128]{1,0:T(8,128)S(1)} %get-tuple-element.46.packed.own_ref), channel_id=1, source_target_pairs={{0,1},{1,0},{2,3},{3,2},{4,5},{5,4},{6,7},{7,6},{8,9},{9,8},{10,11... | collective-permute-start | bytes 86024 | tf_op jit(solution)/shard_map/ppermute | solution.py:492
  3.5 4.4 %collective-permute-start.17 = (f32[56,128]{1,0:T(8,128)S(1)}, f32[56,128]{1,0:T(8,128)S(1)}, u32[]{:S(2)}, u32[]{:S(2)}) collective-permute-start(f32[56,128]{1,0:T(8,128)S(1)} %get-tuple-element.46.packed.own_ref), channel_id=1, source_target_pairs={{0,8},{8,0},{16,24},{24,16},{1,2},{9,10},{17,18},{25,26},{2,1},{10... | collective-permute-start | bytes 86024 | tf_op jit(solution)/shard_map/ppermute | solution.py:493
  8.4 3.8 %collective-permute-start.18 = (f32[40,128]{1,0:T(8,128)S(1)}, f32[40,128]{1,0:T(8,128)S(1)}, u32[]{:S(2)}, u32[]{:S(2)}) collective-permute-start(f32[40,128]{1,0:T(8,128)S(1)} %get-tuple-element.51), channel_id=1, source_target_pairs={{0,8},{8,0},{16,24},{24,16},{1,9},{9,1},{17,25},{25,17},{2,10},{10... | collective-permute-start | bytes 61448 | tf_op jit(solution)/shard_map/ppermute | solution.py:492
  10.4 1.8 %collective-permute-start.19 = (f32[40,128]{1,0:T(8,128)S(1)}, f32[40,128]{1,0:T(8,128)S(1)}, u32[]{:S(2)}, u32[]{:S(2)}) collective-permute-start(f32[40,128]{1,0:T(8,128)S(1)} %get-tuple-element.52), channel_id=1, source_target_pairs={{0,1},{1,0},{2,3},{3,2},{4,5},{5,4},{6,7},{7,6},{8,16},{9,17},{10,... | collective-permute-start | bytes 61448 | tf_op jit(solution)/shard_map/ppermute | solution.py:493
  13.6 14.4 %all-to-all-start = ((f32[32,1,128]{2,1,0:T(1,128)}), f32[32,1,128]{2,1,0:T(1,128)S(1)}, u32[]{:S(2)}, u32[]{:S(2)}) async-start(f32[32,1,128]{2,1,0:T(1,128)} %get-tuple-element.57), calls=%async_computation | async-start | bytes 32768 | tf_op jit(solution)/shard_map/all_to_all | solution.py:600
  22.7 6.2 %copy-start = (f32[96,128]{1,0:T(8,128)S(1)}, f32[96,128]{1,0:T(8,128)}, u32[]{:S(2)}) copy-start(f32[96,128]{1,0:T(8,128)} %fs_hbm.1) | copy-start | bytes 147460
  22.7 6.2 %copy-start.1 = (s32[96,128]{1,0:T(8,128)S(1)}, s32[96,128]{1,0:T(8,128)}, u32[]{:S(2)}) copy-start(s32[96,128]{1,0:T(8,128)} %kmt_hbm.1) | copy-start | bytes 147460

commit v2 on v1

--- a/solution.py
+++ b/solution.py
@@ -31,12 +31,10 @@
     return value if shift == 0 else pltpu.roll(value, shift, axis)
 
 
-def grouped_sum(value, first, last):
-    step = first
-    while step < last:
-        value = value + roll(value, step)
-        step *= 2
-    return value
+def tree_sum(values):
+    while len(values) > 1:
+        values = [sum(values[i : i + 2][1:], values[i]) for i in range(0, len(values), 2)]
+    return values[0]
 
 
 def unfold(block, rows, levels):
@@ -205,25 +203,23 @@
     return jnp.where(index < lax.axis_size(axis) - 1, after, 0.0), jnp.where(index > 0, before, 0.0)
 
 
-def complete(mine, e, w, rhs, levels):
+def complete(mine, e, w, rhs, levels, offset):
     cols = mine.shape[1]
     lane = lanes_of(mine.shape)
-    beyond = jnp.where(lane % 2 == 0, roll(e, -1), roll(w, 1))
-    jump_beyond = roll(beyond, 4 * levels) - roll(beyond, 2 * levels)
-    jump_mine = roll(mine, 4 * levels) - roll(mine, 2 * levels)
-    here = (lane >= 4 * levels) & (lane < 6 * levels)
-    inward = jnp.where(here, mine * jump_beyond, 0.0)
+    even = lane % 2 == 0
+    start = 4 * levels
+    here = (lane >= start) & (lane < 6 * levels)
+    ends = (lane == 0) | (lane == cols - 1)
+    jump_mine = roll(mine, start - offset) - roll(mine, 2 * levels - offset)
+    beyond = jnp.where(even, roll(e, -1 - offset), roll(w, 1 - offset))
+    jump_e = roll(e, start - 1 - offset) - roll(e, 2 * levels - 1 - offset)
+    jump_w = roll(w, start + 1 - offset) - roll(w, 2 * levels + 1 - offset)
+    inward = jnp.where(here, roll(mine, -offset) * jnp.where(even, jump_e, jump_w), 0.0)
     outward = jnp.where(here, beyond * jump_mine, 0.0)
-    both = inward + roll(outward, 2 * levels)
-    both = grouped_sum(both, 2, 2 * levels) / levels
-    ends = (lane == 0) | (lane == cols - 1)
-    rhs = rhs + jnp.where(ends, roll(both, cols - 1 - (6 * levels - 2)), 0.0)
-    base = 6 * levels
-    first = roll(both, base + REACH - (8 * levels - 2))
-    second = roll(both, base + REACH - 1 - (8 * levels - 1))
-    strip = jnp.where(lane % 8 < REACH, w, e)
-    strip = strip + jnp.where(lane == base + REACH, first, 0.0) + jnp.where(lane == base + REACH - 1, second, 0.0)
-    return rhs, strip
+    added = tree_sum([roll(inward, cols - 1 - start - 2 * k) for k in range(levels)]) / levels
+    passed = tree_sum([roll(outward, cols - 2 - start - 2 * k) for k in range(-1, levels)]) / levels
+    strip = roll(jnp.where(lane % 8 < REACH, w, e), cols - REACH - 6 * levels - offset)
+    return rhs + jnp.where(ends, added, 0.0), strip + jnp.where(ends, passed, 0.0)
 
 
 def ends_kernel(got_a, got_b, packed, top, bottom, weight, rhs_in, send_a, send_b, corner_out):
@@ -231,27 +227,28 @@
     levels = top.shape[0] // 3
     east, west = sides("bx", got_a[...], got_b[...])
 
-    def outer_rows(block):
-        last = block[rows // 2 - TILE : rows // 2]
-        return jnp.concatenate([block[:TILE], roll(last, -(6 * levels + 16))], axis=0)
-
-    rhs = jnp.concatenate([rhs_in[pl.ds(0, TILE), :], rhs_in[pl.ds(rows - TILE, TILE), :]], axis=0)
-    rhs, strip = complete(outer_rows(packed[...]), outer_rows(east), outer_rows(west), rhs, levels)
+    ends = []
+    for first, begin, offset in ((0, 0, 0), (rows - TILE, rows // 2 - TILE, 6 * levels + 16)):
+        part = slice(begin, begin + TILE)
+        near = packed[pl.ds(begin, TILE), :]
+        ends.append(complete(near, east[part], west[part], rhs_in[pl.ds(first, TILE), :], levels, offset))
+    (rhs_low, strip_low), (rhs_high, strip_high) = ends
     tile = (TILE, cols)
     corner = jnp.where(lanes_of(tile) % 8 < REACH, west[rows // 2 :], east[rows // 2 :])
-    corner_out[...] = corner
+    corner_out[0] = corner
+    corner_out[1] = roll(corner, 8 * levels)
     row = rows_of(tile)
     first, last = weight[pl.ds(0, TILE), :], weight[pl.ds(rows - TILE, TILE), :]
     n3 = 3 * levels
     above = (
         top[...],
-        jnp.where(row < REACH, roll(last, REACH, 0), rhs[TILE:]),
-        jnp.where(row == 0, corner[1:2], strip[TILE:]),
+        jnp.where(row < REACH, roll(last, REACH, 0), rhs_high),
+        jnp.where(row == 0, corner[1:2], strip_high),
     )
     below = (
         bottom[...],
-        jnp.where(row < REACH, rhs[:TILE], roll(first, REACH, 0)),
-        jnp.where(row == REACH, corner[:1], strip[:TILE]),
+        jnp.where(row < REACH, rhs_low, roll(first, REACH, 0)),
+        jnp.where(row == REACH, corner[:1], strip_low),
     )
     even = is_even("by")
     for ref, one, two in ((send_a, above, below), (send_b, below, above)):
@@ -260,11 +257,11 @@
         ref[pl.ds(n3 + TILE, TILE), :] = jnp.where(even, one[2], two[2])
 
 
-def krylov(rhs_c, heavy_c, strip, heavy_strip):
+def krylov(rhs_c, heavy_c, strip):
     lane = lanes_of(rhs_c.shape)
     cols = rhs_c.shape[1]
     near = (lane < REACH) | (lane >= cols - REACH)
-    rhs_s, heavy_s = jnp.where(near, strip, 0.0), jnp.where(near, heavy_strip, 0.0)
+    rhs_s, heavy_s = jnp.where(near, strip, 0.0), jnp.where(near, roll(strip, -8), 0.0)
     scale = 1.0 / HALFWIDTH
     diag_c, side_c = jnp.where(heavy_c > 0, (heavy_c - CENTER) * scale, 0.0), jnp.where(heavy_c > 0, scale, 0.0)
     diag_s, side_s = jnp.where(heavy_s > 0, (heavy_s - CENTER) * scale, 0.0), jnp.where(heavy_s > 0, scale, 0.0)
@@ -293,20 +290,19 @@
     ]
 
 
-def spread(strip, levels):
-    at = strip.shape[1] - REACH - 6 * levels
-    return roll(strip, at), roll(strip, at - 8)
-
-
 def middle_kernel(got_a, got_b, packed, top, weight, rhs_in, rhs_out, strip_out, basis, sums):
     rows, _ = weight.shape
     levels = top.shape[0] // 3
     east, west = sides("bx", got_a[pl.ds(0, rows // 2), :], got_b[pl.ds(0, rows // 2), :])
     mine = packed[pl.ds(0, rows // 2), :]
-    rhs, strip = complete(*(unfold(v, rows, levels) for v in (mine, east, west)), rhs_in[...], levels)
+    half = rows // 2
+    parts = [
+        complete(mine, east, west, rhs_in[pl.ds(i * half, half), :], levels, i * (6 * levels + 16)) for i in range(2)
+    ]
+    rhs, strip = (jnp.concatenate(pair, axis=0) for pair in zip(*parts))
     rhs_out[...] = rhs
     strip_out[...] = strip
-    vectors = [v[TILE : rows - TILE] for v in krylov(rhs, weight[...], *spread(strip, levels))]
+    vectors = [v[TILE : rows - TILE] for v in krylov(rhs, weight[...], strip)]
     for i, v in enumerate(vectors):
         basis[i] = v
     for i, v in enumerate(products(vectors)):
@@ -330,20 +326,19 @@
     add_bottom = dot(bottom_v[2 * levels :], jump(south[:n3]))
     add_north = dot(north[2 * levels : n3], jump(top_v))
     add_south = dot(south[2 * levels : n3], jump(bottom_v))
-    corner = corner_in[...]
-    low, high = corner[:1], corner[1:2]
+    turned = corner_in[1]
     c_north, c_south = north[n3 + TILE + REACH : n3 + TILE + REACH + 1], south[n3 + TILE : n3 + TILE + 1]
-    half = 8 * levels
     edge = (1, cols)
     lane_1 = lanes_of(edge)
-
-    def cross(coefficient, value):
-        product = jnp.where(lane_1 >= half, coefficient * roll(value, half), 0.0)
-        summed = grouped_sum(product, 8, 8 * levels) / levels
-        return jnp.where((lane_1 // 8) == 6 * levels // 8, roll(summed, 6 * levels - (16 * levels - 8)), 0.0)
-
-    strip_top, strip_bottom = cross(high, c_north), cross(low, c_south)
-    strip_north, strip_south = cross(c_north, high), cross(c_south, low)
+    tile = (TILE, cols)
+    crossed = jnp.where(rows_of(tile) == 0, c_north * turned[1:2], c_south * turned[:1])
+    lower = lanes_of(tile) < 8 * levels
+    near = (lanes_of(tile) < REACH) | (lanes_of(tile) >= cols - REACH)
+    gain, given = jnp.where(lower, crossed, 0.0), jnp.where(lower, 0.0, crossed)
+    gain = tree_sum([roll(gain, cols - REACH - 8 * k) for k in range(levels)]) / levels
+    given = tree_sum([roll(given, cols - REACH - 8 * levels - 8 * k) for k in range(levels)]) / levels
+    gain, given = jnp.where(near, gain, 0.0), jnp.where(near, given, 0.0)
+    strip_top, strip_bottom, strip_north, strip_south = gain[:1], gain[1:2], given[:1], given[1:2]
     outer = rows_of((TILE, cols))
     flat_n, flat_s = north[n3 : n3 + TILE], south[n3 : n3 + TILE]
 
@@ -362,7 +357,7 @@
     heavy_c = bands(weight, roll(flat_s, REACH, 0), roll(flat_n, REACH, 0))
     strip = bands(strip_in, south[n3 + TILE :], north[n3 + TILE :])
     strip = patch(strip, strip_south, strip_bottom, strip_top, strip_north)
-    vectors = krylov(rhs_c, heavy_c, *spread(strip, levels))
+    vectors = krylov(rhs_c, heavy_c, strip)
     vectors = [jnp.concatenate([v[TILE : 2 * TILE], v[4 * TILE : 5 * TILE]], axis=0) for v in vectors]
     line = jnp.zeros(edge, jnp.float32)
     for i, v in enumerate(vectors):
@@ -580,7 +575,7 @@
     deep = lines + 2 * TILE
     send_a, send_b, corner = call(
         ends_kernel,
-        [f32(deep, cols), f32(deep, cols), f32(TILE, cols)],
+        [f32(deep, cols), f32(deep, cols), f32(2, TILE, cols)],
         "v" * 7,
     )(x_a, x_b, packed, top, bottom, weight, rhs)
     y_a, y_b = exchange(send_a, send_b, "by")

time: 29.1 us -> 28.5 us (0.979)
  Pallas kernels: 7.87 us -> 7.19 us
    pallas_call x1, Pallas kernels: 1.46 us -> 1.12 us  [per_device(): call(rows_kernel, [f32(size, 2 * TILE, cols), f32(everyone, 1, cols)], 'v...]
    pallas_call x1, Pallas kernels: 0.48 us -> 0.18 us  [per_device(): call(ends_kernel, [f32(deep, cols), f32(deep, cols), f32(2, TILE, cols)],...]
where the time goes in v2:
time: 28.5 us; the launch traced here: 28.3 us
  starting transfers between devices  12.5 us (44%)
  waiting for transfers between devices  7.96 us (28%)
  Pallas kernels  7.19 us (25%)
  between operations  0.7 us (2%)
    all_to_all x1, starting transfers between devices, per_device(): got = lax.all_to_all(moments, ('by', 'bx'), 0, 0, tiled=True)  7.26 us
    all_to_all x1, waiting for transfers between devices, per_device(): got = lax.all_to_all(moments, ('by', 'bx'), 0, 0, tiled=True)  5.3 us
    ppermute x2, starting transfers between devices, exchange(): got_a = lax.ppermute(first, axis, pairs_a)  2.64 us
    ppermute x2, starting transfers between devices, exchange(): got_b = lax.ppermute(second, axes, pairs_b)  2.55 us
    pallas_call x1, Pallas kernels, per_device(): call(stencil_kernel, [f32(rows // 2 + TILE, cols), f32(lines, cols), f32(...  2.27 us
    ppermute x2, waiting for transfers between devices, exchange(): got_b = lax.ppermute(second, axes, pairs_b)  1.85 us
    pallas_call x1, Pallas kernels, per_device(): call(tracers_kernel, [f32(*tracers.shape)], 'v' * 11, resident=False, cos...  1.79 us
    pallas_call x1, Pallas kernels, per_device(): call(rows_kernel, [f32(size, 2 * TILE, cols), f32(everyone, 1, cols)], 'v...  1.12 us
  transfers between devices with their start and end apart: 5, of which 3 were waited for; matrix products, arithmetic and copies ran while one was open for 0% of the time, Pallas kernels for 10%

profile of v2, /device:TPU:0, one launch (start us, length us, event | category | flops | bytes accessed | tf_op | source)
XLA Modules:
  0.0 28.3 jit_solution(1961257160646888729)
XLA Ops:
  0.6 2.3 %shard_map.85 = (f32[56,128]{1,0:T(8,128)S(1)}, f32[24,128]{1,0:T(8,128)S(1)}, f32[24,128]{1,0:T(8,128)S(1)}, f32[96,128]{1,0:T(8,128)S(1)}, f32[96,128]{1,0:T(8...) custom-call(f32[2,8,96,128]{3,2,1,0:T(8,128)} %tr_hbm.1, ...), custom_call_target="tpu_custom_call" | custom-call | tf_op jit(solution)/shard_map/pallas_call | solution.py:562
  2.9 0.6 %collective-permute-start.16 = (f32[56,128]{1,0:T(8,128)S(1)}, f32[56,128]{1,0:T(8,128)S(1)}, u32[]{:S(2)}, u32[]{:S(2)}) collective-permute-start(f32[56,128]{1,0:T(8,128)S(1)} %get-tuple-element.46.packed.own_ref), channel_id=1, source_target_pairs={{0,1},{1,0},{2,3},{3,2},{4,5},{5,4},{6,7},{7,6},{8,9},{9,8},{10,11... | collective-permute-start | bytes 86024 | tf_op jit(solution)/shard_map/ppermute | solution.py:487
  3.5 2.6 %collective-permute-start.17 = (f32[56,128]{1,0:T(8,128)S(1)}, f32[56,128]{1,0:T(8,128)S(1)}, u32[]{:S(2)}, u32[]{:S(2)}) collective-permute-start(f32[56,128]{1,0:T(8,128)S(1)} %get-tuple-element.46.packed.own_ref), channel_id=1, source_target_pairs={{0,8},{8,0},{16,24},{24,16},{1,2},{9,10},{17,18},{25,26},{2,1},{10... | collective-permute-start | bytes 86024 | tf_op jit(solution)/shard_map/ppermute | solution.py:488
  6.0 0.0 collective-permute-done.16.got_a.east_west_a
  6.0 1.8 %collective-permute-done.17.got_b.east_west_b = f32[56,128]{1,0:T(8,128)S(1)} collective-permute-done((f32[56,128]{1,0:T(8,128)S(1)}, f32[56,128]{1,0:T(8,128)S(1)}, u32[]{:S(2)}, u32[]{:S(2)}) %collective-permute-start.17) | collective-permute-done | bytes 28704 | tf_op jit(solution)/shard_map/ppermute | solution.py:488
  7.9 0.2 shard_map.86
  8.1 2.1 %collective-permute-start.18 = (f32[40,128]{1,0:T(8,128)S(1)}, f32[40,128]{1,0:T(8,128)S(1)}, u32[]{:S(2)}, u32[]{:S(2)}) collective-permute-start(f32[40,128]{1,0:T(8,128)S(1)} %get-tuple-element.51), channel_id=1, source_target_pairs={{0,8},{8,0},{16,24},{24,16},{1,9},{9,1},{17,25},{25,17},{2,10},{10... | collective-permute-start | bytes 61448 | tf_op jit(solution)/shard_map/ppermute | solution.py:487
  10.1 0.0 collective-permute-start.19
  10.1 0.9 %shard_map.88 = (f32[96,128]{1,0:T(8,128)S(1)}, f32[96,128]{1,0:T(8,128)S(1)}, f32[5,80,128]{2,1,0:T(8,128)S(1)}, f32[15,8,128]{2,1,0:T(8,128)S(1)}) custom-call(f32[56,128]{1,0:T(8,128)S(1)} %collective-permute-done.16.got_a.east_west_a, f32[56,128]{1,0:T(8,128)S(1)} %collective-permute-done.17.got_b.east_west_b, ...), custom_call_target="tpu_custom_call" | custom-call | flops 2457600 | bytes 245760 | tf_op jit(solution)/shard_map/pallas_call | solution.py:584
  11.1 0.8 %collective-permute-done.18.north_south_a.got_a = f32[40,128]{1,0:T(8,128)S(1)} collective-permute-done((f32[40,128]{1,0:T(8,128)S(1)}, f32[40,128]{1,0:T(8,128)S(1)}, u32[]{:S(2)}, u32[]{:S(2)}) %collective-permute-start.18) | collective-permute-done | bytes 20512 | tf_op jit(solution)/shard_map/ppermute | solution.py:487
  11.9 0.0 collective-permute-done.19.north_south_b.got_b
  11.9 1.1 %shard_map.89 = (f32[5,16,128]{2,1,0:T(8,128)S(1)}, f32[32,1,128]{2,1,0:T(1,128)}) custom-call(f32[40,128]{1,0:T(8,128)S(1)} %collective-permute-done.18.north_south_a.got_a, f32[40,128]{1,0:T(8,128)S(1)} %collective-permute-done.19.north_south_b.got_b, f32[24,128]{1,0:T(8,128)S(1)} %get-tuple-element.47.top, f32[24,128]{1,0:T(8,128)S(1)} %get-tuple-element.48.bottom, ...), custom_call_target="tpu_custom_call" | custom-call | tf_op jit(solution)/shard_map/pallas_call | solution.py:590
  13.0 7.3 %all-to-all-start = ((f32[32,1,128]{2,1,0:T(1,128)}), f32[32,1,128]{2,1,0:T(1,128)S(1)}, u32[]{:S(2)}, u32[]{:S(2)}) async-start(f32[32,1,128]{2,1,0:T(1,128)} %get-tuple-element.57), calls=%async_computation | async-start | bytes 32768 | tf_op jit(solution)/shard_map/all_to_all | solution.py:595
  20.3 1.8 %shard_map.87 = f32[2,8,96,128]{3,2,1,0:T(8,128)} custom-call(f32[2,8,96,128]{3,2,1,0:T(8,128)S(1)} %get-tuple-element.42.tr, f32[2,8,96,128]{3,2,1,0:T(8,128)S(1)} %get-tuple-element.43.ve, f32[8,96,128]{2,1,0:T(8,128)S(1)} %get-tuple-element.44.di, s32[96,128]{1,0:T(8,128)S(1)} %get-tuple-element.45.kmt_ref, ...), custom_call_target="tpu_custom_call" | custom-call | flops 5898240 | bytes 3145728 | tf_op jit(solution)/shard_map/pallas_call | solution.py:596
  22.1 0.0 copy-start
  22.1 0.0 copy-start.1
  22.1 5.3 %all-to-all-done.got = f32[32,1,128]{2,1,0:T(1,128)S(1)} async-done(((f32[32,1,128]{2,1,0:T(1,128)}), f32[32,1,128]{2,1,0:T(1,128)S(1)}, u32[]{:S(2)}, u32[]{:S(2)}) %all-to-all-start) | async-done | bytes 16416 | tf_op jit(solution)/shard_map/all_to_all | solution.py:595
  27.4 0.9 %shard_map.90 = (f32[96,128]{1,0:T(8,128)}, f32[96,128]{1,0:T(8,128)}, s32[1,1]{1,0:T(1,128)S(4)}) custom-call(f32[32,1,128]{2,1,0:T(1,128)S(1)} %all-to-all-done.got, f32[5,80,128]{2,1,0:T(8,128)S(1)} %get-tuple-element.58.middle, f32[5,16,128]{2,1,0:T(8,128)S(1)} %get-tuple-element.59.outer), custom_call_target="tpu_custom_call" | custom-call | tf_op jit(solution)/shard_map/pallas_call | solution.py:603
  28.3 0.0 copy-done
  28.3 0.0 copy-done.1
  (1 shorter events, 0.0 us)
Async XLA Ops:
  2.9 3.1 %collective-permute-start.16 = (f32[56,128]{1,0:T(8,128)S(1)}, f32[56,128]{1,0:T(8,128)S(1)}, u32[]{:S(2)}, u32[]{:S(2)}) collective-permute-start(f32[56,128]{1,0:T(8,128)S(1)} %get-tuple-element.46.packed.own_ref), channel_id=1, source_target_pairs={{0,1},{1,0},{2,3},{3,2},{4,5},{5,4},{6,7},{7,6},{8,9},{9,8},{10,11... | collective-permute-start | bytes 86024 | tf_op jit(solution)/shard_map/ppermute | solution.py:487
  3.5 4.4 %collective-permute-start.17 = (f32[56,128]{1,0:T(8,128)S(1)}, f32[56,128]{1,0:T(8,128)S(1)}, u32[]{:S(2)}, u32[]{:S(2)}) collective-permute-start(f32[56,128]{1,0:T(8,128)S(1)} %get-tuple-element.46.packed.own_ref), channel_id=1, source_target_pairs={{0,8},{8,0},{16,24},{24,16},{1,2},{9,10},{17,18},{25,26},{2,1},{10... | collective-permute-start | bytes 86024 | tf_op jit(solution)/shard_map/ppermute | solution.py:488
  8.1 3.8 %collective-permute-start.18 = (f32[40,128]{1,0:T(8,128)S(1)}, f32[40,128]{1,0:T(8,128)S(1)}, u32[]{:S(2)}, u32[]{:S(2)}) collective-permute-start(f32[40,128]{1,0:T(8,128)S(1)} %get-tuple-element.51), channel_id=1, source_target_pairs={{0,8},{8,0},{16,24},{24,16},{1,9},{9,1},{17,25},{25,17},{2,10},{10... | collective-permute-start | bytes 61448 | tf_op jit(solution)/shard_map/ppermute | solution.py:487
  10.1 1.8 %collective-permute-start.19 = (f32[40,128]{1,0:T(8,128)S(1)}, f32[40,128]{1,0:T(8,128)S(1)}, u32[]{:S(2)}, u32[]{:S(2)}) collective-permute-start(f32[40,128]{1,0:T(8,128)S(1)} %get-tuple-element.52), channel_id=1, source_target_pairs={{0,1},{1,0},{2,3},{3,2},{4,5},{5,4},{6,7},{7,6},{8,16},{9,17},{10,... | collective-permute-start | bytes 61448 | tf_op jit(solution)/shard_map/ppermute | solution.py:488
  13.0 14.4 %all-to-all-start = ((f32[32,1,128]{2,1,0:T(1,128)}), f32[32,1,128]{2,1,0:T(1,128)S(1)}, u32[]{:S(2)}, u32[]{:S(2)}) async-start(f32[32,1,128]{2,1,0:T(1,128)} %get-tuple-element.57), calls=%async_computation | async-start | bytes 32768 | tf_op jit(solution)/shard_map/all_to_all | solution.py:595
  22.1 6.2 %copy-start = (f32[96,128]{1,0:T(8,128)S(1)}, f32[96,128]{1,0:T(8,128)}, u32[]{:S(2)}) copy-start(f32[96,128]{1,0:T(8,128)} %fs_hbm.1) | copy-start | bytes 147460
  22.1 6.2 %copy-start.1 = (s32[96,128]{1,0:T(8,128)S(1)}, s32[96,128]{1,0:T(8,128)}, u32[]{:S(2)}) copy-start(s32[96,128]{1,0:T(8,128)} %kmt_hbm.1) | copy-start | bytes 147460
